TPU v7x, 256 devices: a whole 4x4x8 slice. The times are simulated.
256 devices in a mesh: layer: 32 (over y, z), row: 2 (over core), col: 4 (over x).
Axes of the slice: x: 4, y: 4, z: 8, core: 2. Of those that a mesh axis runs over, the one named last changes fastest.
Arguments:
- lpanel: bfloat16 [32, 8, 3072, 256], P('layer', None, 'row', 'col'), may hold values from -6 to 6
- upanel: bfloat16 [32, 8, 256, 3072], P('layer', None, 'row', 'col'), may hold values from -0.03125 to 0.03125
- lpat: int32 [32, 8, 24], P('layer', None, 'row'), may hold values 0 or 1
- upat: int32 [32, 8, 24], P('layer', None, 'col'), may hold values 0 or 1
- ancestor_entries: float32 [3072, 3072], P('row', 'col'), may hold values from -2 to 64, as said below
Outputs:
- schur: float32 [3072, 3072], P(('row', 'layer'), 'col')
- diag_lu: float32 [24, 128, 128], P('col')
Inputs may be any that keep to these rules, and one draw needn't show every extreme that they name: `ancestor_entries`: entries on the diagonal lie in 32 to 64; all other entries in -2 to 2.
All inputs are finite; a program needn't handle non-finite values. No bound on the sum of `lpat` or of `upat` on one device may be relied on, other than what follows from the above.
Results may differ from a plain program's by a relative error of at most 0.0003.
Values may be sent and summed in bfloat16 or wider, within the bound.
A program may use at most 64 MiB of HBM per device.

v0:
```python
import jax
import jax.numpy as jnp
from jax import lax
from jax.sharding import PartitionSpec as P

BLK = 128
panel_width = 16


def mask_rows(panel, pattern, block):
    count, length, inner = panel.shape
    shaped = panel.reshape(count, length // block, block, inner)
    return (shaped * pattern[:, :, None, None].astype(panel.dtype)).reshape(count, length, inner)


def mask_cols(panel, pattern, block):
    count, inner, length = panel.shape
    shaped = panel.reshape(count, inner, length // block, block)
    return (shaped * pattern[:, None, :, None].astype(panel.dtype)).reshape(count, inner, length)


def eliminate_tall(tile, steps):
    row_places = jnp.arange(tile.shape[1])
    col_places = jnp.arange(tile.shape[2])

    def eliminate_sweep(step, current):
        pivot = current[:, step, step]
        below = row_places > step
        column = jnp.where(below[None, :], current[:, :, step] / pivot[:, None], 0.0)
        right = col_places > step
        row_part = jnp.where(right[None, :], current[:, step, :], 0.0)
        current = current - column[:, :, None] * row_part[:, None, :]
        placed = below[None, :, None] & (col_places == step)[None, None, :]
        return jnp.where(placed, column[:, :, None], current)

    return lax.fori_loop(0, steps, eliminate_sweep, tile)


def forward_rows(unit, strip):
    places = jnp.arange(unit.shape[1])

    def forward_sweep(step, current):
        factors = jnp.where(places[None, :] > step, unit[:, :, step], 0.0)
        return current - factors[:, :, None] * current[:, step, :][:, None, :]

    return lax.fori_loop(0, unit.shape[1], forward_sweep, strip)


def factor(blocks):
    size = blocks.shape[-1]
    current = blocks
    for offset in range(0, size, panel_width):
        end = offset + panel_width
        panel = eliminate_tall(current[:, offset:, offset:end], panel_width)
        current = current.at[:, offset:, offset:end].set(panel)
        if end < size:
            strip = forward_rows(panel[:, :panel_width, :], current[:, offset:end, end:])
            current = current.at[:, offset:end, end:].set(strip)
            lower = panel[:, panel_width:, :]
            trailing = current[:, end:, end:] - jnp.einsum(
                "bik,bkj->bij",
                lower,
                strip,
                precision=lax.Precision.HIGHEST,
                preferred_element_type=jnp.float32,
            )
            current = current.at[:, end:, end:].set(trailing)
    return current


def candidates(matrix):
    width = matrix.shape[1]
    per_group = lax.axis_size("col") // lax.axis_size("row")
    column = lax.axis_index("col")
    valid = column // per_group == lax.axis_index("row")
    begin = column % per_group * width
    square = lax.dynamic_slice_in_dim(matrix, begin, width, 0)
    count = width // BLK
    blocks = jnp.stack(
        [square[j * BLK : (j + 1) * BLK, j * BLK : (j + 1) * BLK] for j in range(count)]
    )
    return (blocks, valid)


def pick_owned(gathered):
    per_group = lax.axis_size("col") // lax.axis_size("row")
    count = gathered.shape[0] // lax.axis_size("row")
    source = lax.axis_index("col") // per_group
    return lax.dynamic_slice_in_dim(gathered, source * count, count, 0)


def shards(lpanel, upanel, lpat, upat, ancestor_entries):
    left_masked = mask_rows(lpanel[0], lpat[0], BLK)
    right_masked = mask_cols(upanel[0], upat[0], BLK)
    right_full = lax.all_gather(right_masked, "row", axis=1, tiled=True)
    length = left_masked.shape[1]
    update = jnp.einsum(
        "kmw,kwn->mn",
        lax.all_gather(left_masked, "col", axis=2, tiled=True),
        right_full,
        preferred_element_type=jnp.float32,
    )
    share_rows = length // lax.axis_size("layer")
    offset = lax.axis_index("layer") * share_rows
    total = lax.psum(update, "layer")
    summed = ancestor_entries - total
    schur = lax.dynamic_slice_in_dim(summed, offset, share_rows, 0)
    pivots, valid = candidates(summed)
    diag_lu = factor(pick_owned(lax.all_gather(pivots, "row", axis=0, tiled=True)))
    return (schur, diag_lu)


def solution(mesh):
    return jax.shard_map(
        shards,
        mesh=mesh,
        in_specs=(
            P("layer", None, "row", "col"),
            P("layer", None, "row", "col"),
            P("layer", None, "row"),
            P("layer", None, "col"),
            P("row", "col"),
        ),
        out_specs=(P(("row", "layer"), "col"), P("col", None, None)),
        check_vma=False,
    )
```

profile of v0, /device:TPU:1, one launch (start us, length us, event | category | flops | bytes accessed | tf_op | source)
XLA Modules:
  0.0 484.4 jit_solution(14656002472003928525)
XLA Ops:
  7.2 0.9 copy.122
  8.3 2.7 bitcast_multiply_fusion
  11.2 1.4 bitcast_multiply_fusion.1
  12.6 20.4 %all-gather.5.cloned.1.call-done = bf16[8,256,768]{2,1,0:T(8,128)(2,1)} async-done(((bf16[8,128,768]{2,1,0:T(8,128)(2,1)}), bf16[8,256,768]{2,1,0:T(8,128)(2,1)}) %all-gather.5.cloned.1.call-update) | async-done | bytes 3145744 | tf_op jit(solution)/shard_map/all_gather | solution.py:95
  33.1 70.4 %all-gather.3.cloned.1.call-done = bf16[8,1536,256]{1,2,0:T(8,128)(2,1)} async-done(((bf16[8,1536,64]{1,2,0:T(8,128)(2,1)}), bf16[8,1536,256]{1,2,0:T(8,128)(2,1)}) %all-gather.3.cloned.1.call-update) | async-done | bytes 6291472 | tf_op jit(solution)/shard_map/all_gather | solution.py:99
  103.5 9.7 %convolution_bitcast_fusion = f32[1536,768]{1,0:T(8,128)} fusion(bf16[8,1536,256]{1,2,0:T(8,128)(2,1)} %all-gather.3.cloned.1.call-done, bf16[8,256,768]{2,1,0:T(8,128)(2,1)} %all-gather.5.cloned.1.call-done), kind=kOutput, calls=%fused_computation.119 | convolution fusion | flops 4831838208 | bytes 14155776 | tf_op jit(solution)/shard_map/kmw,kwn->mn/dot_general | solution.py:97
  114.6 166.0 %all-reduce.2.cloned.1.call-done = f32[1536,768]{1,0:T(8,128)} async-done(((f32[1536,768]{1,0:T(8,128)}), f32[1536,768]{1,0:T(8,128)}) %all-reduce.2.cloned.1.call-update) | async-done | bytes 4718608 | tf_op jit(solution)/shard_map/psum | solution.py:105
  280.6 4.4 sub.134
  285.1 3.9 all_gather.11
  289.3 13.2 %while.248 = (s32[]{:T(128)}, f32[6,128,16]{1,0,2:T(8,128)S(1)}, s32[]{:T(128)}) while((s32[]{:T(128)}, f32[6,128,16]{1,0,2:T(8,128)S(1)}, s32[]{:T(128)}) %tuple.580), condition=%wide.region_2.3_spmd.clone.clone, body=%wide.region_1.2_spmd.clone.clone.sunk | while | flops 40706 | bytes 212433 | solution.py:36
  302.6 2.6 while.241
  305.4 2.1 dynamic-slice_select_fusion
  307.4 6.4 %scatter.75 = f32[6,128,128]{1,2,0:T(8,128)S(1)} dynamic-update-slice(f32[6,128,128]{1,2,0:T(8,128)S(1)} %get-tuple-element.1863, f32[6,16,112]{1,2,0:T(8,128)S(1)} %dynamic-slice_select_fusion, s32[]{:T(128)} %constant.1116.clone.1, s32[]{:T(128)} %bitcast.13, s32[]{:T(128)} %bitcast.14) | dynamic-update-slice | bytes 86020 | tf_op jit(solution)/shard_map/scatter | solution.py:58
  314.6 7.3 %scatter.76 = f32[6,128,128]{1,2,0:T(8,128)S(1)} dynamic-update-slice(f32[6,128,128]{1,2,0:T(8,128)S(1)} %scatter.75, f32[6,112,112]{1,2,0:T(8,128)S(1)} %convolution_subtract_fusion, s32[]{:T(128)} %constant.1116.clone.1, s32[]{:T(128)} %constant.1125.clone.1, s32[]{:T(128)} %constant.1125.clone.1) | dynamic-update-slice | bytes 602116 | tf_op jit(solution)/shard_map/scatter | solution.py:67
  322.0 12.9 %while.249 = (s32[]{:T(128)}, f32[6,112,16]{1,0,2:T(8,128)S(1)}, s32[]{:T(128)}) while((s32[]{:T(128)}, f32[6,112,16]{1,0,2:T(8,128)S(1)}, s32[]{:T(128)}) %tuple.586), condition=%wide.region_7.8_spmd.clone.clone, body=%wide.region_6.7_spmd.clone.clone.sunk | while | flops 35634 | bytes 186145 | solution.py:36
  334.9 2.3 scatter.79
  337.4 2.5 while.242
  340.1 3.2 scatter.80
  344.0 3.2 scatter.81
  347.3 12.5 %while.250 = (s32[]{:T(128)}, f32[6,96,16]{1,0,2:T(8,128)S(1)}, s32[]{:T(128)}) while((s32[]{:T(128)}, f32[6,96,16]{1,0,2:T(8,128)S(1)}, s32[]{:T(128)}) %tuple.592), condition=%wide.region_11.12_spmd.clone.clone, body=%wide.region_10.11_spmd.clone.clone.sunk | while | flops 30562 | bytes 159857 | solution.py:36
  359.9 2.3 scatter.84
  362.4 2.6 while.243
  365.1 3.0 scatter.85
  368.7 3.0 scatter.86
  371.8 12.1 %while.251 = (s32[]{:T(128)}, f32[6,80,16]{1,0,2:T(8,128)S(1)}, s32[]{:T(128)}) while((s32[]{:T(128)}, f32[6,80,16]{1,0,2:T(8,128)S(1)}, s32[]{:T(128)}) %tuple.598), condition=%wide.region_15.16_spmd.clone.clone, body=%wide.region_14.15_spmd.clone.clone.sunk | while | flops 25490 | bytes 133569 | solution.py:36
  383.9 2.3 scatter.89
  386.4 2.5 while.244
  389.1 3.0 scatter.90
  392.7 2.8 scatter.91
  395.6 11.8 %while.252 = (s32[]{:T(128)}, f32[6,64,16]{1,0,2:T(8,128)S(1)}, s32[]{:T(128)}) while((s32[]{:T(128)}, f32[6,64,16]{1,0,2:T(8,128)S(1)}, s32[]{:T(128)}) %tuple.604), condition=%wide.region_19.20_spmd.clone.clone, body=%wide.region_18.19_spmd.clone.clone.sunk | while | flops 20418 | bytes 107281 | solution.py:36
  407.4 2.3 scatter.94
  409.8 2.5 while.245
  412.5 2.6 scatter.95
  415.6 2.6 scatter.96
  418.3 11.5 %while.253 = (s32[]{:T(128)}, f32[6,48,16]{1,0,2:T(8,128)S(1)}, s32[]{:T(128)}) while((s32[]{:T(128)}, f32[6,48,16]{1,0,2:T(8,128)S(1)}, s32[]{:T(128)}) %tuple.610), condition=%wide.region_23.24_spmd.clone.clone, body=%wide.region_22.23_spmd.clone.clone.sunk | while | flops 15346 | bytes 80993 | solution.py:36
  429.8 2.3 scatter.99
  432.3 2.5 while.246
  434.9 2.4 scatter.100
  437.8 2.4 scatter.101
  440.2 11.1 %while.254 = (s32[]{:T(128)}, f32[6,32,16]{1,0,2:T(8,128)S(1)}, s32[]{:T(128)}) while((s32[]{:T(128)}, f32[6,32,16]{1,0,2:T(8,128)S(1)}, s32[]{:T(128)}) %tuple.616), condition=%wide.region_27.28_spmd.clone.clone, body=%wide.region_26.27_spmd.clone.clone.sunk | while | flops 10274 | bytes 54705 | solution.py:36
  451.5 2.3 scatter.104
  454.0 3.8 while.247
  457.8 2.2 scatter.105
  460.2 2.2 scatter.106
  462.5 1.6 constant_dynamic-slice_fusion.7
  464.0 10.7 %while.255 = (s32[]{:T(128)}, f32[6,16,16]{1,0,2:T(8,128)S(1)}, s32[]{:T(128)}) while((s32[]{:T(128)}, f32[6,16,16]{1,0,2:T(8,128)S(1)}, s32[]{:T(128)}) %tuple.622), condition=%wide.region_31.32_spmd.clone.clone, body=%wide.region_30.31_spmd.clone.clone.sunk | while | flops 5186 | bytes 28397 | solution.py:36
  474.8 2.2 scatter.109
  477.0 0.9 copy.164
  (1779 shorter events, 111.6 us)
Async XLA Ops:
  7.2 3.8 copy-start.2
  7.2 4.0 copy-start.1
  7.2 25.9 %all-gather.5.cloned.1.call-start = ((), (), s32[]{:S(2)}) async-start(), calls=%async_computation.1 | async-start | bytes 4718592 | tf_op jit(solution)/shard_map/all_gather | solution.py:95
  11.0 92.5 %all-gather.3.cloned.1.call-start = ((), (), s32[]{:S(2)}) async-start(), calls=%async_computation | async-start | bytes 7864320 | tf_op jit(solution)/shard_map/all_gather | solution.py:99
  12.6 268.0 %all-reduce.2.cloned.1.call-start = ((), (), s32[]{:S(2)}) async-start(), calls=%async_computation.2 | async-start | bytes 9437184 | tf_op jit(solution)/shard_map/psum | solution.py:105
  113.2 0.7 copy-start.3
  285.0 4.1 copy-start
Sparse Core Ops, SparseCore 0:
  11.1 21.9 all-gather.4
  34.9 68.5 all-gather.2
  113.3 167.2 all-reduce.1
where the time goes:
time: 485 us; the launch traced here: 484 us
  waiting for transfers between devices  257 us (53%)
  local copies, waits for them, and re-layouts  128 us (26%)
  other arithmetic  55.7 us (11%)
  between operations  14.5 us (3%)
  matrix products  13.4 us (3%)
  loops' own time  11.6 us (2%)
    psum x1, waiting for transfers between devices, shards(): total = lax.psum(update, 'layer')  166 us
    all_gather x1, waiting for transfers between devices, shards(): lax.all_gather(left_masked, 'col', axis=2, tiled=True)  70.4 us
    scatter x7, local copies, waits for them, and re-layouts, factor(): current = current.at[:, end:, end:].set(trailing)  23.7 us
    dynamic_slice x128, local copies, waits for them, and re-layouts, eliminate_sweep(): pivot = current[:, step, step]  23.6 us
    scatter x7, local copies, waits for them, and re-layouts, factor(): current = current.at[:, offset:end, end:].set(strip)  22.9 us
    while x224, local copies, waits for them, and re-layouts  22 us
    all_gather x1, waiting for transfers between devices, shards(): right_full = lax.all_gather(right_masked, 'row', axis=1, tiled=True)  20.4 us
    scatter x8, local copies, waits for them, and re-layouts, factor(): current = current.at[:, offset:, offset:end].set(panel)  16 us
  transfers between devices with their start and end apart: 3, of which 3 were waited for; matrix products, arithmetic and copies ran while one was open for 1% of the time, Pallas kernels for 0%

commit v1 on v0

--- a/solution.py
+++ b/solution.py
@@ -5,6 +5,14 @@
 
 BLK = 128
 panel_width = 16
+
+
+def add_in_pairs(array, name):
+    devices, acc = (lax.axis_size(name), array)
+    for reach in [1 << k for k in range(devices.bit_length() - 1)]:
+        swap = [(i, i ^ reach) for i in range(devices)]
+        acc = acc + lax.ppermute(acc, name, swap)
+    return acc
 
 
 def mask_rows(panel, pattern, block):
@@ -102,7 +110,7 @@
     )
     share_rows = length // lax.axis_size("layer")
     offset = lax.axis_index("layer") * share_rows
-    total = lax.psum(update, "layer")
+    total = add_in_pairs(update, "layer")
     summed = ancestor_entries - total
     schur = lax.dynamic_slice_in_dim(summed, offset, share_rows, 0)
     pivots, valid = candidates(summed)

time: 485 us -> 1050 us (2.16)
  waiting for transfers between devices: 257 us -> 798 us
  starting transfers between devices: 0.12 us -> 14.3 us
    ppermute x0 -> x5, waiting for transfers between devices: none -> 707 us  [add_in_pairs(): acc = acc + lax.ppermute(acc, name, swap)]
    psum x1 -> x0, waiting for transfers between devices: 166 us -> none  [shards(): total = lax.psum(update, 'layer')]
    ppermute x0 -> x5, starting transfers between devices: none -> 14.2 us  [add_in_pairs(): acc = acc + lax.ppermute(acc, name, swap)]
  transfers between devices with their start and end apart: 3 -> 7, of which waited for: 3 -> 7; matrix products, arithmetic and copies ran while one was open for 1% -> 0% of each run, Pallas kernels for 0% -> 0%
where the time goes in v1:
time: 1050 us
  waiting for transfers between devices  798 us (76%)
  local copies, waits for them, and re-layouts  128 us (12%)
  other arithmetic  61.9 us (6%)
  between operations  14.8 us (1%)
  starting transfers between devices  14.3 us (1%)
  matrix products  12 us (1%)
  loops' own time  11.6 us (1%)
    ppermute x5, waiting for transfers between devices, add_in_pairs(): acc = acc + lax.ppermute(acc, name, swap)  707 us
    all_gather x1, waiting for transfers between devices, shards(): lax.all_gather(left_masked, 'col', axis=2, tiled=True)  70.4 us
    scatter x7, local copies, waits for them, and re-layouts, factor(): current = current.at[:, end:, end:].set(trailing)  23.7 us
    dynamic_slice x128, local copies, waits for them, and re-layouts, eliminate_sweep(): pivot = current[:, step, step]  23.6 us
    scatter x7, local copies, waits for them, and re-layouts, factor(): current = current.at[:, offset:end, end:].set(strip)  22.9 us
    while x224, local copies, waits for them, and re-layouts  22 us
  transfers between devices with their start and end apart: 7, of which 7 were waited for; matrix products, arithmetic and copies ran while one was open for 0% of the time, Pallas kernels for 0%

profile of v1, /device:TPU:1, one launch (start us, length us, event | category | flops | bytes accessed | tf_op | source)
XLA Modules:
  0.0 1045.8 jit_solution(8522815536300240366)
XLA Ops:
  8.3 2.7 bitcast_multiply_fusion
  12.5 20.6 %all-gather.5.cloned.1.call-done = bf16[8,256,768]{2,1,0:T(8,128)(2,1)} async-done(((bf16[8,128,768]{2,1,0:T(8,128)(2,1)}), bf16[8,256,768]{2,1,0:T(8,128)(2,1)}) %all-gather.5.cloned.1.call-update) | async-done | bytes 3145744 | tf_op jit(solution)/shard_map/all_gather | solution.py:103
  33.1 70.4 %all-gather.3.cloned.1.call-done = bf16[8,1536,256]{1,2,0:T(8,128)(2,1)} async-done(((bf16[8,1536,64]{1,2,0:T(8,128)(2,1)}), bf16[8,1536,256]{1,2,0:T(8,128)(2,1)}) %all-gather.3.cloned.1.call-update) | async-done | bytes 6291472 | tf_op jit(solution)/shard_map/all_gather | solution.py:107
  103.5 8.3 convolution_bitcast_fusion
  113.2 101.2 %collective-permute-done = f32[1536,768]{1,0:T(8,128)S(1)} collective-permute-done((f32[1536,768]{1,0:T(8,128)S(1)}, f32[1536,768]{1,0:T(8,128)S(1)}, u32[]{:S(2)}, u32[]{:S(2)}) %collective-permute-start) | collective-permute-done | bytes 4718624 | tf_op jit(solution)/shard_map/ppermute | solution.py:14
  215.0 2.4 collective-permute-start.1
  217.4 202.5 %collective-permute-done.1 = f32[1536,768]{1,0:T(8,128)S(1)} collective-permute-done((f32[1536,768]{1,0:T(8,128)S(1)}, f32[1536,768]{1,0:T(8,128)S(1)}, u32[]{:S(2)}, u32[]{:S(2)}) %collective-permute-start.1) | collective-permute-done | bytes 4718624 | tf_op jit(solution)/shard_map/ppermute | solution.py:14
  420.4 6.4 collective-permute-start.2
  426.9 203.5 %collective-permute-done.2 = f32[1536,768]{1,0:T(8,128)S(1)} collective-permute-done((f32[1536,768]{1,0:T(8,128)S(1)}, f32[1536,768]{1,0:T(8,128)S(1)}, u32[]{:S(2)}, u32[]{:S(2)}) %collective-permute-start.2) | collective-permute-done | bytes 4718624 | tf_op jit(solution)/shard_map/ppermute | solution.py:14
  632.2 100.8 %collective-permute-done.3 = f32[1536,768]{1,0:T(8,128)S(1)} collective-permute-done((f32[1536,768]{1,0:T(8,128)S(1)}, f32[1536,768]{1,0:T(8,128)S(1)}, u32[]{:S(2)}, u32[]{:S(2)}) %collective-permute-start.3) | collective-permute-done | bytes 4718624 | tf_op jit(solution)/shard_map/ppermute | solution.py:14
  733.0 2.7 add.456
  735.7 2.7 collective-permute-start.4
  739.9 98.7 %collective-permute-done.4 = f32[1536,768]{1,0:T(8,128)} collective-permute-done((f32[1536,768]{1,0:T(8,128)}, f32[1536,768]{1,0:T(8,128)}, u32[]{:S(2)}, u32[]{:S(2)}) %collective-permute-start.4) | collective-permute-done | bytes 4718624 | tf_op jit(solution)/shard_map/ppermute | solution.py:14
  838.6 6.0 add_subtract_fusion
  844.8 5.3 all_gather.11
  850.3 13.2 %while.248 = (s32[]{:T(128)}, f32[6,128,16]{1,0,2:T(8,128)S(1)}, s32[]{:T(128)}) while((s32[]{:T(128)}, f32[6,128,16]{1,0,2:T(8,128)S(1)}, s32[]{:T(128)}) %tuple.580), condition=%wide.region_1.2_spmd.clone.clone, body=%wide.region_0.1_spmd.clone.clone.sunk | while | flops 40706 | bytes 212433 | solution.py:44
  863.7 2.6 while.241
  868.5 6.4 scatter.75
  875.7 7.3 scatter.76
  883.1 12.9 %while.249 = (s32[]{:T(128)}, f32[6,112,16]{1,0,2:T(8,128)S(1)}, s32[]{:T(128)}) while((s32[]{:T(128)}, f32[6,112,16]{1,0,2:T(8,128)S(1)}, s32[]{:T(128)}) %tuple.586), condition=%wide.region_6.7_spmd.clone.clone, body=%wide.region_5.6_spmd.clone.clone.sunk | while | flops 35634 | bytes 186145 | solution.py:44
  896.0 2.3 scatter.79
  898.5 2.5 while.242
  901.2 3.2 scatter.80
  905.1 3.2 scatter.81
  908.4 12.5 %while.250 = (s32[]{:T(128)}, f32[6,96,16]{1,0,2:T(8,128)S(1)}, s32[]{:T(128)}) while((s32[]{:T(128)}, f32[6,96,16]{1,0,2:T(8,128)S(1)}, s32[]{:T(128)}) %tuple.592), condition=%wide.region_10.11_spmd.clone.clone, body=%wide.region_9.10_spmd.clone.clone.sunk | while | flops 30562 | bytes 159857 | solution.py:44
  920.9 2.3 scatter.84
  923.5 2.6 while.243
  926.1 3.0 scatter.85
  929.8 3.0 scatter.86
  932.9 12.1 %while.251 = (s32[]{:T(128)}, f32[6,80,16]{1,0,2:T(8,128)S(1)}, s32[]{:T(128)}) while((s32[]{:T(128)}, f32[6,80,16]{1,0,2:T(8,128)S(1)}, s32[]{:T(128)}) %tuple.598), condition=%wide.region_14.15_spmd.clone.clone, body=%wide.region_13.14_spmd.clone.clone.sunk | while | flops 25490 | bytes 133569 | solution.py:44
  945.0 2.3 scatter.89
  947.5 2.5 while.244
  950.2 3.0 scatter.90
  953.8 2.8 scatter.91
  956.6 11.8 %while.252 = (s32[]{:T(128)}, f32[6,64,16]{1,0,2:T(8,128)S(1)}, s32[]{:T(128)}) while((s32[]{:T(128)}, f32[6,64,16]{1,0,2:T(8,128)S(1)}, s32[]{:T(128)}) %tuple.604), condition=%wide.region_18.19_spmd.clone.clone, body=%wide.region_17.18_spmd.clone.clone.sunk | while | flops 20418 | bytes 107281 | solution.py:44
  968.5 2.3 scatter.94
  970.9 2.5 while.245
  973.6 2.6 scatter.95
  976.7 2.6 scatter.96
  979.4 11.5 %while.253 = (s32[]{:T(128)}, f32[6,48,16]{1,0,2:T(8,128)S(1)}, s32[]{:T(128)}) while((s32[]{:T(128)}, f32[6,48,16]{1,0,2:T(8,128)S(1)}, s32[]{:T(128)}) %tuple.610), condition=%wide.region_22.23_spmd.clone.clone, body=%wide.region_21.22_spmd.clone.clone.sunk | while | flops 15346 | bytes 80993 | solution.py:44
  990.9 2.3 scatter.99
  993.3 2.5 while.246
  996.0 2.4 scatter.100
  998.8 2.4 scatter.101
  1001.3 11.1 %while.254 = (s32[]{:T(128)}, f32[6,32,16]{1,0,2:T(8,128)S(1)}, s32[]{:T(128)}) while((s32[]{:T(128)}, f32[6,32,16]{1,0,2:T(8,128)S(1)}, s32[]{:T(128)}) %tuple.616), condition=%wide.region_26.27_spmd.clone.clone, body=%wide.region_25.26_spmd.clone.clone.sunk | while | flops 10274 | bytes 54705 | solution.py:44
  1012.6 2.3 scatter.104
  1015.0 3.8 while.247
  1025.1 10.7 %while.255 = (s32[]{:T(128)}, f32[6,16,16]{1,0,2:T(8,128)S(1)}, s32[]{:T(128)}) while((s32[]{:T(128)}, f32[6,16,16]{1,0,2:T(8,128)S(1)}, s32[]{:T(128)}) %tuple.622), condition=%wide.region_30.31_spmd.clone.clone, body=%wide.region_29.30_spmd.clone.clone.sunk | while | flops 5186 | bytes 28397 | solution.py:44
  (1790 shorter events, 129.4 us)
Async XLA Ops:
  7.2 3.9 copy-start.2
  7.2 4.1 copy-start.1
  7.2 25.9 %all-gather.5.cloned.1.call-start = ((), (), s32[]{:S(2)}) async-start(), calls=%async_computation.1 | async-start | bytes 4718592 | tf_op jit(solution)/shard_map/all_gather | solution.py:103
  11.0 92.5 %all-gather.3.cloned.1.call-start = ((), (), s32[]{:S(2)}) async-start(), calls=%async_computation | async-start | bytes 7864320 | tf_op jit(solution)/shard_map/all_gather | solution.py:107
  111.8 102.6 %collective-permute-start = (f32[1536,768]{1,0:T(8,128)S(1)}, f32[1536,768]{1,0:T(8,128)S(1)}, u32[]{:S(2)}, u32[]{:S(2)}) collective-permute-start(f32[1536,768]{1,0:T(8,128)S(1)} %convolution_bitcast_fusion), channel_id=1, source_target_pairs={{0,8},{8,0},{16,24},{24,16},{32,40},{40,32},{48,56},{56,48},{64,72... | collective-permute-start | bytes 14155784 | tf_op jit(solution)/shard_map/ppermute | solution.py:14
  215.0 204.8 %collective-permute-start.1 = (f32[1536,768]{1,0:T(8,128)S(1)}, f32[1536,768]{1,0:T(8,128)S(1)}, u32[]{:S(2)}, u32[]{:S(2)}) collective-permute-start(f32[1536,768]{1,0:T(8,128)S(1)} %add.453), channel_id=1, source_target_pairs={{0,16},{8,24},{16,0},{24,8},{32,48},{40,56},{48,32},{56,40},{64,80... | collective-permute-start | bytes 14155784 | tf_op jit(solution)/shard_map/ppermute | solution.py:14
  420.4 209.9 %collective-permute-start.2 = (f32[1536,768]{1,0:T(8,128)S(1)}, f32[1536,768]{1,0:T(8,128)S(1)}, u32[]{:S(2)}, u32[]{:S(2)}) collective-permute-start(f32[1536,768]{1,0:T(8,128)S(1)} %add.454), channel_id=1, source_target_pairs={{0,32},{8,40},{16,48},{24,56},{32,0},{40,8},{48,16},{56,24},{64,96... | collective-permute-start | bytes 14155784 | tf_op jit(solution)/shard_map/ppermute | solution.py:14
  630.9 108.2 %copy-start.3 = (s32[3]{0:T(128)S(1)}, s32[3]{0:T(128)}, u32[]{:S(2)}) copy-start(s32[3]{0:T(128)} %constant.1126.clone.1) | copy-start | bytes 40
  630.9 102.0 %collective-permute-start.3 = (f32[1536,768]{1,0:T(8,128)S(1)}, f32[1536,768]{1,0:T(8,128)S(1)}, u32[]{:S(2)}, u32[]{:S(2)}) collective-permute-start(f32[1536,768]{1,0:T(8,128)S(1)} %add.455), channel_id=1, source_target_pairs={{0,64},{8,72},{16,80},{24,88},{32,96},{40,104},{48,112},{56,120},{... | collective-permute-start | bytes 14155784 | tf_op jit(solution)/shard_map/ppermute | solution.py:14
  735.7 102.9 %collective-permute-start.4 = (f32[1536,768]{1,0:T(8,128)}, f32[1536,768]{1,0:T(8,128)}, u32[]{:S(2)}, u32[]{:S(2)}) collective-permute-start(f32[1536,768]{1,0:T(8,128)} %add.456), channel_id=1, source_target_pairs={{0,128},{8,136},{16,144},{24,152},{32,160},{40,168},{48,176},{56,1... | collective-permute-start | bytes 14155784 | tf_op jit(solution)/shard_map/ppermute | solution.py:14
  844.6 5.5 copy-start
Sparse Core Ops, SparseCore 0:
  11.1 21.9 all-gather.4
  34.9 68.5 all-gather.2
